TPU v7x, 32 devices: a whole 2x2x4 slice. The times are simulated.
32 devices in a mesh: rows: 8 (over z, core), feat: 4 (over y, x).
Axes of the slice: x: 2, y: 2, z: 4, core: 2. Of those that a mesh axis runs over, the one named last changes fastest.
Arguments:
- features: float32 [8192, 2048], P('rows', 'feat'), may hold values from -200 to 200
- targets: float32 [8192, 2048], P('rows', 'feat'), may hold values from -2000 to 2000
Outputs:
- coefficients: float32 [2048, 2048], P('feat')
- residual: float32 [8192, 2048], P('rows', 'feat')
All inputs are finite; a program needn't handle non-finite values.
Results may differ from a plain program's by a relative error of at most 0.0003.
Values sent between devices are 32-bit elements; how exact they have to be, the bound alone decides.
A program may use at most 64 MiB of HBM per device.

v0:
```python
import jax
import jax.numpy as jnp
from jax import lax
from jax.sharding import PartitionSpec as P

SWEEPS = 1


def shifted(block, axis, distance):
    devices = range(lax.axis_size(axis))
    route = [((i - distance) % len(devices), i) for i in devices]
    return lax.ppermute(block, axis, route)


def on_device(features, targets):
    hi = lax.Precision.HIGHEST
    nblocks = lax.axis_size("feat")
    owner = lax.axis_index("feat")
    width = features.shape[1]
    group_width = targets.shape[1]
    local_gram = lax.dot_general(
        features,
        features,
        (((0,), (0,)), ((), ())),
        precision=hi,
        preferred_element_type=jnp.float32,
    )
    gram = lax.psum(local_gram, "rows")
    lower = jnp.linalg.cholesky(gram)

    def apply_solve(product):
        return jax.scipy.linalg.cho_solve((lower, True), product)

    coef = jnp.zeros((width, group_width * nblocks), jnp.float32)

    def section(s, carry):
        coef, res = carry
        group = (owner - s) % nblocks
        product = lax.dot_general(
            features,
            res,
            (((0,), (0,)), ((), ())),
            precision=hi,
            preferred_element_type=jnp.float32,
        )
        share = lax.psum_scatter(product, "rows", scatter_dimension=1, tiled=True)
        step_part = apply_solve(share)
        step = lax.all_gather(step_part, "rows", axis=1, tiled=True)
        start = group * group_width
        old = lax.dynamic_slice_in_dim(coef, start, group_width, 1)
        coef = lax.dynamic_update_slice_in_dim(coef, old + step, start, 1)
        res = res - jnp.dot(features, step, precision=hi, preferred_element_type=jnp.float32)
        res = shifted(res, "feat", 1)
        return (coef, res)

    coef, residual = lax.fori_loop(0, SWEEPS * nblocks, section, (coef, targets))
    return (coef, residual)


def solution(mesh):
    return jax.shard_map(
        on_device,
        mesh=mesh,
        in_specs=(P("rows", "feat"), P("rows", "feat")),
        out_specs=(P("feat", None), P("rows", "feat")),
        check_vma=False,
    )
```

profile of v0, /device:TPU:0, one launch (start us, length us, event | category | flops | bytes accessed | tf_op | source)
XLA Modules:
  0.0 704.7 jit_solution(12615588743031769837)
XLA Ops:
  7.2 6.8 fusion.62
  16.2 60.1 %all-reduce.3.cloned.1.call-done = f32[512,512]{0,1:T(8,128)} async-done(((f32[512,512]{0,1:T(8,128)}), f32[512,512]{0,1:T(8,128)}) %all-reduce.3.cloned.1.call-update) | async-done | bytes 1048592 | tf_op jit(solution)/shard_map/psum | solution.py:28
  78.2 11.7 %cholesky.104 = f32[128,128]{1,0:T(8,128)S(1)} custom-call(f32[128,128]{1,0:T(8,128)S(1)} %cholesky.266), custom_call_target="Cholesky" | custom-call | tf_op jit(solution)/shard_map/jit(cholesky)/cholesky | solution.py:29
  89.9 9.8 %custom-call.44 = f32[1,128,128]{1,2,0:T(8,128)S(1)} custom-call(f32[1,128,128]{2,1,0:T(8,128)S(1)} %get-tuple-element.297), custom_call_target="InvertDiagBlocksLowerTriangular" | custom-call | tf_op jit(solution)/shard_map/jit(cholesky)/cholesky | solution.py:29
  100.5 11.7 %cholesky.217 = f32[128,128]{1,0:T(8,128)S(1)} custom-call(f32[128,128]{1,0:T(8,128)S(1)} %cholesky.270), custom_call_target="Cholesky" | custom-call | tf_op jit(solution)/shard_map/jit(cholesky)/cholesky | solution.py:29
  112.3 10.0 %custom-call.45 = f32[1,128,128]{1,2,0:T(8,128)S(1)} custom-call(f32[1,128,128]{2,1,0:T(8,128)S(1)} %get-tuple-element.294), custom_call_target="InvertDiagBlocksLowerTriangular" | custom-call | tf_op jit(solution)/shard_map/jit(cholesky)/cholesky | solution.py:29
  123.0 11.7 %cholesky.238 = f32[128,128]{1,0:T(8,128)S(1)} custom-call(f32[128,128]{1,0:T(8,128)S(1)} %cholesky.275), custom_call_target="Cholesky" | custom-call | tf_op jit(solution)/shard_map/jit(cholesky)/cholesky | solution.py:29
  135.4 9.8 %custom-call.46 = f32[1,128,128]{1,2,0:T(8,128)S(1)} custom-call(f32[1,128,128]{2,1,0:T(8,128)S(1)} %get-tuple-element.291), custom_call_target="InvertDiagBlocksLowerTriangular" | custom-call | tf_op jit(solution)/shard_map/jit(cholesky)/cholesky | solution.py:29
  145.8 11.7 %cholesky.255 = f32[128,128]{1,0:T(8,128)S(1)} custom-call(f32[128,128]{1,0:T(8,128)S(1)} %convolution_subtract_fusion.8), custom_call_target="Cholesky" | custom-call | tf_op jit(solution)/shard_map/jit(cholesky)/cholesky | solution.py:29
  162.8 7.6 %while.22 = (s32[]{:T(128)}, f32[512,512]{1,0:T(8,128)S(1)}, s32[4,2]{0,1:T(2,128)S(1)}, f32[4,128,128]{2,1,0:T(8,128)S(1)}, s32[]{:T(128)}) while((s32[]{:T(128)}, f32[512,512]{1,0:T(8,128)S(1)}, s32[4,2]{0,1:T(2,128)S(1)}, f32[4,128,128]{2,1,0:T(8,128)S(1)}, s32[]{:T(128)}) %tuple.76), condition=%wide.while_cond, body=%wide.while_body.sunk | while | flops 2 | bytes 131189 | solution.py:32
  170.4 39.3 %custom-call.47 = f32[4,128,128]{1,2,0:T(8,128)S(1)} custom-call(f32[4,128,128]{2,1,0:T(8,128)S(1)} %get-tuple-element.252), custom_call_target="InvertDiagBlocksLowerTriangular" | custom-call | tf_op jit(solution)/shard_map/while/body/eval_jaxpr/jit(_cho_solve)/triangular_solve | solution.py:32
  212.4 482.4 %while.21 = (s32[]{:T(128)}, f32[512,2048]{1,0:T(8,128)}, f32[1024,512]{0,1:T(8,128)}, s32[]{:T(128)}, f32[1024,512]{1,0:T(8,128)S(1)}, /*index=5*/f32[4,128,128...) while((s32[]{:T(128)}, f32[512,2048]{1,0:T(8,128)}, ...), condition=%wide.region_11.12_spmd, body=%wide.region_9.11_spmd.sunk | while | flops 6695698432 | bytes 48759232 | solution.py:56
  212.4 6.1 fusion.150
  219.9 30.4 %reduce-scatter.2.cloned.1.call-done = f32[512,64]{0,1:T(8,128)} async-done(((f32[512,512]{0,1:T(8,128)}), f32[512,64]{0,1:T(8,128)}) %reduce-scatter.2.cloned.1.call-update) | async-done | bytes 131088 | tf_op jit(solution)/shard_map/while/body/eval_jaxpr/reduce_scatter | solution.py:46
  257.4 20.6 %all-gather.2.cloned.1.call-done = f32[512,512]{0,1:T(8,128)} async-done(((f32[512,64]{0,1:T(8,128)}), f32[512,512]{0,1:T(8,128)}) %all-gather.2.cloned.1.call-update) | async-done | bytes 1048592 | tf_op jit(solution)/shard_map/while/body/eval_jaxpr/all_gather | solution.py:48
  278.0 6.2 bitcast_subtract_fusion.2
  295.7 37.5 %collective-permute-done = f32[1024,512]{0,1:T(8,128)} collective-permute-done((f32[1024,512]{0,1:T(8,128)}, f32[1024,512]{0,1:T(8,128)}, u32[]{:S(2)}, u32[]{:S(2)}) %collective-permute-start) | collective-permute-done | bytes 2097184 | tf_op jit(solution)/shard_map/while/body/eval_jaxpr/ppermute | solution.py:12
  333.3 6.1 fusion.150
  340.8 30.1 %reduce-scatter.2.cloned.1.call-done = f32[512,64]{0,1:T(8,128)} async-done(((f32[512,512]{0,1:T(8,128)}), f32[512,64]{0,1:T(8,128)}) %reduce-scatter.2.cloned.1.call-update) | async-done | bytes 131088 | tf_op jit(solution)/shard_map/while/body/eval_jaxpr/reduce_scatter | solution.py:46
  377.9 20.5 %all-gather.2.cloned.1.call-done = f32[512,512]{0,1:T(8,128)} async-done(((f32[512,64]{0,1:T(8,128)}), f32[512,512]{0,1:T(8,128)}) %all-gather.2.cloned.1.call-update) | async-done | bytes 1048592 | tf_op jit(solution)/shard_map/while/body/eval_jaxpr/all_gather | solution.py:48
  398.5 6.2 bitcast_subtract_fusion.2
  416.1 37.5 %collective-permute-done = f32[1024,512]{0,1:T(8,128)} collective-permute-done((f32[1024,512]{0,1:T(8,128)}, f32[1024,512]{0,1:T(8,128)}, u32[]{:S(2)}, u32[]{:S(2)}) %collective-permute-start) | collective-permute-done | bytes 2097184 | tf_op jit(solution)/shard_map/while/body/eval_jaxpr/ppermute | solution.py:12
  453.7 6.1 fusion.150
  461.2 30.0 %reduce-scatter.2.cloned.1.call-done = f32[512,64]{0,1:T(8,128)} async-done(((f32[512,512]{0,1:T(8,128)}), f32[512,64]{0,1:T(8,128)}) %reduce-scatter.2.cloned.1.call-update) | async-done | bytes 131088 | tf_op jit(solution)/shard_map/while/body/eval_jaxpr/reduce_scatter | solution.py:46
  498.3 20.8 %all-gather.2.cloned.1.call-done = f32[512,512]{0,1:T(8,128)} async-done(((f32[512,64]{0,1:T(8,128)}), f32[512,512]{0,1:T(8,128)}) %all-gather.2.cloned.1.call-update) | async-done | bytes 1048592 | tf_op jit(solution)/shard_map/while/body/eval_jaxpr/all_gather | solution.py:48
  519.1 6.2 bitcast_subtract_fusion.2
  536.8 37.6 %collective-permute-done = f32[1024,512]{0,1:T(8,128)} collective-permute-done((f32[1024,512]{0,1:T(8,128)}, f32[1024,512]{0,1:T(8,128)}, u32[]{:S(2)}, u32[]{:S(2)}) %collective-permute-start) | collective-permute-done | bytes 2097184 | tf_op jit(solution)/shard_map/while/body/eval_jaxpr/ppermute | solution.py:12
  574.4 6.1 fusion.150
  581.9 30.1 %reduce-scatter.2.cloned.1.call-done = f32[512,64]{0,1:T(8,128)} async-done(((f32[512,512]{0,1:T(8,128)}), f32[512,64]{0,1:T(8,128)}) %reduce-scatter.2.cloned.1.call-update) | async-done | bytes 131088 | tf_op jit(solution)/shard_map/while/body/eval_jaxpr/reduce_scatter | solution.py:46
  619.0 20.6 %all-gather.2.cloned.1.call-done = f32[512,512]{0,1:T(8,128)} async-done(((f32[512,64]{0,1:T(8,128)}), f32[512,512]{0,1:T(8,128)}) %all-gather.2.cloned.1.call-update) | async-done | bytes 1048592 | tf_op jit(solution)/shard_map/while/body/eval_jaxpr/all_gather | solution.py:48
  639.6 6.2 bitcast_subtract_fusion.2
  657.3 37.5 %collective-permute-done = f32[1024,512]{0,1:T(8,128)} collective-permute-done((f32[1024,512]{0,1:T(8,128)}, f32[1024,512]{0,1:T(8,128)}, u32[]{:S(2)}, u32[]{:S(2)}) %collective-permute-start) | collective-permute-done | bytes 2097184 | tf_op jit(solution)/shard_map/while/body/eval_jaxpr/ppermute | solution.py:12
  (159 shorter events, 101.9 us)
Async XLA Ops:
  7.2 6.9 copy-start.3
  7.2 69.1 %all-reduce.3.cloned.1.call-start = ((), (), s32[]{:S(2)}) async-start(), calls=%async_computation.1 | async-start | bytes 2097152 | tf_op jit(solution)/shard_map/psum | solution.py:28
  76.3 1.7 copy-start.2
  209.9 2.5 copy-start
  212.4 37.9 %reduce-scatter.2.cloned.1.call-start = ((), (), s32[]{:S(2)}) async-start(), calls=%async_computation.2 | async-start | bytes 1179648 | tf_op jit(solution)/shard_map/while/body/eval_jaxpr/reduce_scatter | solution.py:46
  218.5 59.5 %all-gather.2.cloned.1.call-start = ((), (), s32[]{:S(2)}) async-start(), calls=%async_computation.3 | async-start | bytes 1179648 | tf_op jit(solution)/shard_map/while/body/eval_jaxpr/all_gather | solution.py:48
  284.3 49.0 %collective-permute-start = (f32[1024,512]{0,1:T(8,128)}, f32[1024,512]{0,1:T(8,128)}, u32[]{:S(2)}, u32[]{:S(2)}) collective-permute-start(f32[1024,512]{0,1:T(8,128)} %bitcast_subtract_fusion.2), channel_id=1, source_target_pairs={{3,0},{0,1},{1,2},{2,3},{7,4},{4,5},{5,6},{6,7},{11,8},{8,9},{9,10... | collective-permute-start | bytes 6291464 | tf_op jit(solution)/shard_map/while/body/eval_jaxpr/ppermute | solution.py:12
  285.7 4.9 copy-start.1
  333.3 37.6 %reduce-scatter.2.cloned.1.call-start = ((), (), s32[]{:S(2)}) async-start(), calls=%async_computation.2 | async-start | bytes 1179648 | tf_op jit(solution)/shard_map/while/body/eval_jaxpr/reduce_scatter | solution.py:46
  339.4 59.1 %all-gather.2.cloned.1.call-start = ((), (), s32[]{:S(2)}) async-start(), calls=%async_computation.3 | async-start | bytes 1179648 | tf_op jit(solution)/shard_map/while/body/eval_jaxpr/all_gather | solution.py:48
  404.7 49.0 %collective-permute-start = (f32[1024,512]{0,1:T(8,128)}, f32[1024,512]{0,1:T(8,128)}, u32[]{:S(2)}, u32[]{:S(2)}) collective-permute-start(f32[1024,512]{0,1:T(8,128)} %bitcast_subtract_fusion.2), channel_id=1, source_target_pairs={{3,0},{0,1},{1,2},{2,3},{7,4},{4,5},{5,6},{6,7},{11,8},{8,9},{9,10... | collective-permute-start | bytes 6291464 | tf_op jit(solution)/shard_map/while/body/eval_jaxpr/ppermute | solution.py:12
  406.2 4.9 copy-start.1
  453.7 37.5 %reduce-scatter.2.cloned.1.call-start = ((), (), s32[]{:S(2)}) async-start(), calls=%async_computation.2 | async-start | bytes 1179648 | tf_op jit(solution)/shard_map/while/body/eval_jaxpr/reduce_scatter | solution.py:46
  459.8 59.3 %all-gather.2.cloned.1.call-start = ((), (), s32[]{:S(2)}) async-start(), calls=%async_computation.3 | async-start | bytes 1179648 | tf_op jit(solution)/shard_map/while/body/eval_jaxpr/all_gather | solution.py:48
  525.4 49.0 %collective-permute-start = (f32[1024,512]{0,1:T(8,128)}, f32[1024,512]{0,1:T(8,128)}, u32[]{:S(2)}, u32[]{:S(2)}) collective-permute-start(f32[1024,512]{0,1:T(8,128)} %bitcast_subtract_fusion.2), channel_id=1, source_target_pairs={{3,0},{0,1},{1,2},{2,3},{7,4},{4,5},{5,6},{6,7},{11,8},{8,9},{9,10... | collective-permute-start | bytes 6291464 | tf_op jit(solution)/shard_map/while/body/eval_jaxpr/ppermute | solution.py:12
  526.9 4.9 copy-start.1
  574.4 37.6 %reduce-scatter.2.cloned.1.call-start = ((), (), s32[]{:S(2)}) async-start(), calls=%async_computation.2 | async-start | bytes 1179648 | tf_op jit(solution)/shard_map/while/body/eval_jaxpr/reduce_scatter | solution.py:46
  580.5 59.1 %all-gather.2.cloned.1.call-start = ((), (), s32[]{:S(2)}) async-start(), calls=%async_computation.3 | async-start | bytes 1179648 | tf_op jit(solution)/shard_map/while/body/eval_jaxpr/all_gather | solution.py:48
  645.8 49.0 %collective-permute-start = (f32[1024,512]{0,1:T(8,128)}, f32[1024,512]{0,1:T(8,128)}, u32[]{:S(2)}, u32[]{:S(2)}) collective-permute-start(f32[1024,512]{0,1:T(8,128)} %bitcast_subtract_fusion.2), channel_id=1, source_target_pairs={{3,0},{0,1},{1,2},{2,3},{7,4},{4,5},{5,6},{6,7},{11,8},{8,9},{9,10... | collective-permute-start | bytes 6291464 | tf_op jit(solution)/shard_map/while/body/eval_jaxpr/ppermute | solution.py:12
  647.3 4.9 copy-start.1
Sparse Core Ops, SparseCore 0:
  14.2 62.0 all-reduce.2
  218.6 31.6 reduce-scatter.1
  257.6 20.4 all-gather.1
  339.5 31.3 reduce-scatter.1
  378.1 20.3 all-gather.1
  459.9 31.2 reduce-scatter.1
  498.4 20.6 all-gather.1
  580.6 31.2 reduce-scatter.1
  619.1 20.4 all-gather.1
where the time goes:
time: 710 us; the launch traced here: 705 us
  waiting for transfers between devices  414 us (58%)
  other arithmetic  137 us (19%)
  matrix products  83.3 us (12%)
  local copies, waits for them, and re-layouts  47 us (7%)
  between operations  16.8 us (2%)
    ppermute x4, waiting for transfers between devices, shifted(): return lax.ppermute(block, axis, route)  150 us
    reduce_scatter x4, waiting for transfers between devices, section(): share = lax.psum_scatter(product, 'rows', scatter_dimension=1, tiled=True)  121 us
    all_gather x4, waiting for transfers between devices, section(): step = lax.all_gather(step_part, 'rows', axis=1, tiled=True)  82.5 us
    another operation x14, other arithmetic, on_device(): lower = jnp.linalg.cholesky(gram)  78.6 us
    psum x1, waiting for transfers between devices, on_device(): gram = lax.psum(local_gram, 'rows')  60.1 us
    another operation x11, other arithmetic, apply_solve(): return jax.scipy.linalg.cho_solve((lower, True), product)  48.8 us
    another operation x56, matrix products, apply_solve(): return jax.scipy.linalg.cho_solve((lower, True), product)  25.3 us
    dot_general x4, matrix products, section(): jnp.dot(features, step, precision=hi, preferred_element_type=jnp.float32)  25 us
  transfers between devices with their start and end apart: 13, of which 13 were waited for; matrix products, arithmetic and copies ran while one was open for 7% of the time, Pallas kernels for 0%

commit v1 on v0

v1 whole, which is shorter than its diff:
```python
import functools

import jax
import jax.numpy as jnp
from jax import lax
from jax.experimental import pallas as pl
from jax.experimental.pallas import tpu as pltpu
from jax.sharding import PartitionSpec as P

SWEEPS = 1
HI = lax.Precision.HIGHEST
GATHER_BYTES = 16 * 2**20


def shifted(block, axis, distance):
    devices = range(lax.axis_size(axis))
    route = [((i - distance) % len(devices), i) for i in devices]
    return lax.ppermute(block, axis, route)


def invert_tile(m):
    n = m.shape[0]
    lane = lax.broadcasted_iota(jnp.int32, (8, n), 1)
    sub = lax.broadcasted_iota(jnp.int32, (8, n), 0)
    lanes = lax.broadcasted_iota(jnp.int32, (n, n), 1)
    for q in range(n // 8):
        c = 8 * q
        panel = m[c : c + 8, :]
        d = [jnp.broadcast_to(panel[:, c + t : c + t + 1], (8, n)) for t in range(8)]
        mine = (lane >= c) & (lane < c + 8)
        panel = jnp.where(mine, jnp.where(lane - c == sub, 1.0, 0.0), panel)
        for t in range(8):
            inv = 1.0 / d[t][t : t + 1, :]
            row = panel[t : t + 1, :] * inv
            panel = jnp.where(sub == t, row, panel - d[t] * row)
            for u in range(t + 1, 8):
                head = d[u][t : t + 1, :] * inv
                d[u] = jnp.where(sub == t, head, d[u] - d[t] * head)
        new = jnp.where((lanes >= c) & (lanes < c + 8), 0.0, m)
        for t in range(8):
            new = new - jnp.broadcast_to(m[:, c + t : c + t + 1], (n, n)) * panel[t : t + 1, :]
        parts = [new[:c, :]] if q else []
        parts.append(panel)
        if c + 8 < n:
            parts.append(new[c + 8 :, :])
        m = jnp.concatenate(parts, axis=0)
    return m


def invert_kernel(tile, a_ref, o_ref):
    n = a_ref.shape[0]
    o_ref[...] = a_ref[...]
    eye = jnp.where(
        lax.broadcasted_iota(jnp.int32, (tile, tile), 0)
        == lax.broadcasted_iota(jnp.int32, (tile, tile), 1),
        1.0,
        0.0,
    )

    def block(k, _):
        at = pl.ds(pl.multiple_of(k * tile, tile), tile)
        pivot = invert_tile(o_ref[at, at])
        column = o_ref[:, at]
        o_ref[at, at] = eye
        row = jnp.dot(pivot, o_ref[at, :], precision=HI, preferred_element_type=jnp.float32)
        o_ref[:, at] = jnp.zeros((n, tile), jnp.float32)
        o_ref[...] -= jnp.dot(column, row, precision=HI, preferred_element_type=jnp.float32)
        o_ref[at, :] = row
        return 0

    lax.fori_loop(0, n // tile, block, 0)


def invert(gram):
    n = gram.shape[0]
    return pl.pallas_call(
        functools.partial(invert_kernel, min(128, n)),
        out_shape=jax.ShapeDtypeStruct((n, n), jnp.float32),
        in_specs=[pl.BlockSpec(memory_space=pltpu.VMEM)],
        out_specs=pl.BlockSpec(memory_space=pltpu.VMEM),
        cost_estimate=pl.CostEstimate(
            flops=2 * n**3 * 20, bytes_accessed=8 * n * n, transcendentals=0
        ),
    )(gram)


def tmul(a, b, precision):
    return lax.dot_general(
        a, b, (((0,), (0,)), ((), ())), precision=precision, preferred_element_type=jnp.float32
    )


def gathered(features, targets):
    high = lax.Precision.HIGH
    nblocks = lax.axis_size("feat")
    owner = lax.axis_index("feat")
    width = features.shape[1]
    group_width = targets.shape[1]
    gram = lax.psum(tmul(features, features, HI), "rows")
    blocks = [features] + [shifted(features, "feat", -s) for s in range(1, nblocks)]
    inverse = invert(gram)
    inverses = [inverse] + [shifted(inverse, "feat", -s) for s in range(1, nblocks)]
    res = targets
    coef = jnp.zeros((width, group_width * nblocks), jnp.float32)
    for s in range(nblocks):
        product = tmul(blocks[s], res, high)
        share = lax.psum_scatter(product, "rows", scatter_dimension=1, tiled=True)
        part = jnp.dot(inverses[s], share, precision=HI, preferred_element_type=jnp.float32)
        step = lax.all_gather(part, "rows", axis=1, tiled=True)
        res = res - jnp.dot(blocks[s], step, precision=high, preferred_element_type=jnp.float32)
        back = shifted(step, "feat", s) if s else step
        start = ((owner - s) % nblocks) * group_width
        coef = lax.dynamic_update_slice_in_dim(coef, back, start, 1)
    return (coef, res)


def general(features, targets):
    nblocks = lax.axis_size("feat")
    owner = lax.axis_index("feat")
    width = features.shape[1]
    group_width = targets.shape[1]
    inverse = invert(lax.psum(tmul(features, features, HI), "rows"))
    coef = jnp.zeros((width, group_width * nblocks), jnp.float32)

    def section(s, carry):
        coef, res = carry
        group = (owner - s) % nblocks
        product = tmul(features, res, HI)
        share = lax.psum_scatter(product, "rows", scatter_dimension=1, tiled=True)
        part = jnp.dot(inverse, share, precision=HI, preferred_element_type=jnp.float32)
        step = lax.all_gather(part, "rows", axis=1, tiled=True)
        start = group * group_width
        old = lax.dynamic_slice_in_dim(coef, start, group_width, 1)
        coef = lax.dynamic_update_slice_in_dim(coef, old + step, start, 1)
        res = res - jnp.dot(features, step, precision=HI, preferred_element_type=jnp.float32)
        res = shifted(res, "feat", 1)
        return (coef, res)

    return lax.fori_loop(0, SWEEPS * nblocks, section, (coef, targets))


def on_device(features, targets):
    nblocks = lax.axis_size("feat")
    if SWEEPS == 1 and nblocks * features.size * 4 <= GATHER_BYTES:
        return gathered(features, targets)
    return general(features, targets)


def solution(mesh):
    return jax.shard_map(
        on_device,
        mesh=mesh,
        in_specs=(P("rows", "feat"), P("rows", "feat")),
        out_specs=(P("feat", None), P("rows", "feat")),
        check_vma=False,
    )
```

time: 710 us -> 438 us (0.62)
  other arithmetic: 137 us -> 0 us
  waiting for transfers between devices: 414 us -> 311 us
  local copies, waits for them, and re-layouts: 47 us -> 17.1 us
  matrix products: 83.3 us -> 54.4 us
  Pallas kernels: 0 us -> 22.3 us
  starting transfers between devices: 6.09 us -> 18.6 us
    another operation x25 -> x0, other arithmetic: 127 us -> none  [the longest x14 78.6 us: on_device(): lower = jnp.linalg.cholesky(gram)]
    reduce_scatter x4 -> x3, waiting for transfers between devices: 121 us -> 36.8 us  [gathered(): share = lax.psum_scatter(product, 'rows', scatter_dimension=1, tiled=True)]
    another operation x62 -> x0, matrix products: 27.2 us -> none  [the longest x56 25.3 us: apply_solve(): return jax.scipy.linalg.cho_solve((lower, True), product)]
    pallas_call x0 -> x1, Pallas kernels: none -> 22.3 us  [invert(): pl.pallas_call(functools.partial(invert_kernel, min(128, n)), out_shape=j...]
    dynamic_slice x8 -> x0, local copies, waits for them, and re-layouts: 19.7 us -> none  [section(): old = lax.dynamic_slice_in_dim(coef, start, group_width, 1)]
    ppermute x4 -> x9, waiting for transfers between devices: 150 us -> 135 us  [shifted(): return lax.ppermute(block, axis, route)]
    all_gather x4, waiting for transfers between devices: 82.5 us -> 69.9 us  [gathered(): step = lax.all_gather(part, 'rows', axis=1, tiled=True)]
    ppermute x4 -> x9, starting transfers between devices: 5.87 us -> 18.2 us  [shifted(): return lax.ppermute(block, axis, route)]
  transfers between devices with their start and end apart: 13 -> 18, of which waited for: 13 -> 16; matrix products, arithmetic and copies ran while one was open for 7% -> 8% of each run, Pallas kernels for 0% -> 5%
where the time goes in v1:
time: 438 us
  waiting for transfers between devices  311 us (71%)
  matrix products  54.4 us (12%)
  Pallas kernels  22.3 us (5%)
  starting transfers between devices  18.6 us (4%)
  local copies, waits for them, and re-layouts  17.1 us (4%)
  between operations  14 us (3%)
    ppermute x9, waiting for transfers between devices, shifted(): return lax.ppermute(block, axis, route)  135 us
    all_gather x4, waiting for transfers between devices, gathered(): step = lax.all_gather(part, 'rows', axis=1, tiled=True)  69.9 us
    psum x1, waiting for transfers between devices, gathered(): gram = lax.psum(tmul(features, features, HI), 'rows')  57.6 us
    reduce_scatter x3, waiting for transfers between devices, gathered(): share = lax.psum_scatter(product, 'rows', scatter_dimension=1, tiled=True)  36.8 us
    pallas_call x1, Pallas kernels, invert(): pl.pallas_call(functools.partial(invert_kernel, min(128, n)), out_shape=j...  22.3 us
    dot_general x4, matrix products, tmul(): lax.dot_general(a, b, (((0,), (0,)), ((), ())), precision=precision, pref...  20.2 us
    ppermute x9, starting transfers between devices, shifted(): return lax.ppermute(block, axis, route)  18.2 us
    dot_general x4, matrix products, gathered(): jnp.dot(blocks[s], step, precision=high, preferred_element_type=jnp.float32)  17.7 us
  transfers between devices with their start and end apart: 18, of which 16 were waited for; matrix products, arithmetic and copies ran while one was open for 8% of the time, Pallas kernels for 5%

profile of v1, /device:TPU:0, one launch (start us, length us, event | category | flops | bytes accessed | tf_op | source)
XLA Modules:
  0.0 437.9 jit_solution(6612493872131973703)
XLA Ops:
  7.2 6.8 %fusion.2 = f32[512,512]{1,0:T(8,128)} fusion(f32[1024,512]{1,0:T(8,128)} %param.2), kind=kOutput, calls=%fused_computation.14 | convolution fusion | flops 3221225472 | bytes 3145728 | tf_op jit(solution)/shard_map/dot_general | solution.py:88
  14.1 4.4 %convolution_bitcast_fusion.3 = f32[512,512]{1,0:T(8,128)} fusion(f32[1024,512]{1,0:T(8,128)S(1)} %copy-done, f32[1024,512]{1,0:T(8,128)} %param.3), kind=kOutput, calls=%fused_computation.7 | convolution fusion | flops 1610612736 | bytes 5242880
  18.6 57.6 %all-reduce.2.cloned.1.call-done.a_ref = f32[512,512]{1,0:T(8,128)} async-done(((f32[512,512]{1,0:T(8,128)}), f32[512,512]{1,0:T(8,128)}) %all-reduce.2.cloned.1.call-update) | async-done | bytes 1048592 | tf_op jit(solution)/shard_map/psum | solution.py:99
  76.2 22.3 %shard_map.41 = f32[512,512]{1,0:T(8,128)} custom-call(f32[512,512]{1,0:T(8,128)} %all-reduce.2.cloned.1.call-done.a_ref), custom_call_target="tpu_custom_call" | custom-call | flops 5368709120 | bytes 2097152 | tf_op jit(solution)/shard_map/pallas_call | solution.py:76
  98.6 11.8 %reduce-scatter.13.cloned.1.call-done = f32[64,512]{1,0:T(8,128)} async-done(((f32[512,512]{1,0:T(8,128)}), f32[64,512]{1,0:T(8,128)}) %reduce-scatter.13.cloned.1.call-update) | async-done | bytes 131088
  110.3 3.0 fusion
  116.0 2.9 copy.11
  118.8 15.0 %all-gather.5.cloned.1.call-done = f32[512,512]{0,1:T(8,128)} async-done(((f32[512,64]{0,1:T(8,128)}), f32[512,512]{0,1:T(8,128)}) %all-gather.5.cloned.1.call-update) | async-done | bytes 1048592 | tf_op jit(solution)/shard_map/all_gather | solution.py:109
  133.8 3.9 bitcast_subtract_fusion.3
  137.8 19.9 %collective-permute-done.1 = f32[1024,512]{1,0:T(8,128)} collective-permute-done((f32[1024,512]{1,0:T(8,128)S(1)}, f32[1024,512]{1,0:T(8,128)}, u32[]{:S(2)}, u32[]{:S(2)}) %collective-permute-start.1) | collective-permute-done | bytes 2097184 | tf_op jit(solution)/shard_map/ppermute | solution.py:18
  157.7 4.4 %convolution_bitcast_fusion.2 = f32[512,512]{0,1:T(8,128)} fusion(f32[1024,512]{0,1:T(8,128)S(1)} %bitcast_subtract_fusion.3, f32[1024,512]{1,0:T(8,128)} %collective-permute-done.1), kind=kOutput, calls=%fused_computation.6 | convolution fusion | flops 1610612736 | bytes 5242880 | tf_op jit(solution)/shard_map/dot_general | solution.py:88
  162.2 3.5 collective-permute-start
  165.7 18.4 %collective-permute-done = f32[512,512]{1,0:T(8,128)} collective-permute-done((f32[512,512]{1,0:T(8,128)S(1)}, f32[512,512]{1,0:T(8,128)}, u32[]{:S(2)}, u32[]{:S(2)}) %collective-permute-start) | collective-permute-done | bytes 1048608 | tf_op jit(solution)/shard_map/ppermute | solution.py:18
  184.1 13.2 %reduce-scatter.7.cloned.1.call-done = f32[512,64]{0,1:T(8,128)} async-done(((f32[512,512]{0,1:T(8,128)}), f32[512,64]{0,1:T(8,128)}) %reduce-scatter.7.cloned.1.call-update) | async-done | bytes 131088 | tf_op jit(solution)/shard_map/reduce_scatter | solution.py:107
  197.3 3.0 fusion.3
  202.1 19.0 %all-gather.7.cloned.1.call-done = f32[512,512]{0,1:T(8,128)} async-done(((f32[512,64]{0,1:T(8,128)}), f32[512,512]{0,1:T(8,128)}) %all-gather.7.cloned.1.call-update) | async-done | bytes 1048592 | tf_op jit(solution)/shard_map/all_gather | solution.py:109
  221.1 4.5 %bitcast_subtract_fusion.2 = f32[1024,512]{0,1:T(8,128)S(1)} fusion(f32[1024,512]{0,1:T(8,128)} %copy-done.4, f32[512,512]{0,1:T(8,128)} %all-gather.7.cloned.1.call-done, f32[1024,512]{1,0:T(8,128)} %collective-permute-done.1), kind=kOutput, calls=%fused_computation.2 | convolution fusion | flops 1611137024 | bytes 7340032 | tf_op jit(solution)/shard_map/dot_general | solution.py:110
  225.6 19.1 %collective-permute-done.4 = f32[1024,512]{1,0:T(8,128)} collective-permute-done((f32[1024,512]{1,0:T(8,128)S(1)}, f32[1024,512]{1,0:T(8,128)}, u32[]{:S(2)}, u32[]{:S(2)}) %collective-permute-start.4) | collective-permute-done | bytes 2097184 | tf_op jit(solution)/shard_map/ppermute | solution.py:18
  244.7 4.4 %convolution_bitcast_fusion.1 = f32[512,512]{0,1:T(8,128)} fusion(f32[1024,512]{0,1:T(8,128)S(1)} %bitcast_subtract_fusion.2, f32[1024,512]{1,0:T(8,128)} %collective-permute-done.4), kind=kOutput, calls=%fused_computation.5 | convolution fusion | flops 1610612736 | bytes 5242880 | tf_op jit(solution)/shard_map/dot_general | solution.py:88
  251.0 19.3 %collective-permute-done.3 = f32[512,512]{1,0:T(8,128)} collective-permute-done((f32[512,512]{1,0:T(8,128)S(1)}, f32[512,512]{1,0:T(8,128)}, u32[]{:S(2)}, u32[]{:S(2)}) %collective-permute-start.3) | collective-permute-done | bytes 1048608 | tf_op jit(solution)/shard_map/ppermute | solution.py:18
  270.3 12.7 %reduce-scatter.9.cloned.1.call-done = f32[512,64]{0,1:T(8,128)} async-done(((f32[512,512]{0,1:T(8,128)}), f32[512,64]{0,1:T(8,128)}) %reduce-scatter.9.cloned.1.call-update) | async-done | bytes 131088 | tf_op jit(solution)/shard_map/reduce_scatter | solution.py:107
  283.0 3.0 fusion.4
  288.1 18.6 %all-gather.9.cloned.1.call-done = f32[512,512]{0,1:T(8,128)} async-done(((f32[512,64]{0,1:T(8,128)}), f32[512,512]{0,1:T(8,128)}) %all-gather.9.cloned.1.call-update) | async-done | bytes 1048592 | tf_op jit(solution)/shard_map/all_gather | solution.py:109
  306.6 4.5 %bitcast_subtract_fusion.1 = f32[1024,512]{0,1:T(8,128)S(1)} fusion(f32[1024,512]{0,1:T(8,128)} %copy-done.3, f32[512,512]{0,1:T(8,128)} %all-gather.9.cloned.1.call-done, f32[1024,512]{1,0:T(8,128)} %collective-permute-done.4), kind=kOutput, calls=%fused_computation.1 | convolution fusion | flops 1611137024 | bytes 7340032 | tf_op jit(solution)/shard_map/dot_general | solution.py:110
  311.2 20.6 %collective-permute-done.7 = f32[1024,512]{1,0:T(8,128)} collective-permute-done((f32[1024,512]{1,0:T(8,128)S(1)}, f32[1024,512]{1,0:T(8,128)}, u32[]{:S(2)}, u32[]{:S(2)}) %collective-permute-start.7) | collective-permute-done | bytes 2097184 | tf_op jit(solution)/shard_map/ppermute | solution.py:18
  331.8 4.5 %convolution_bitcast_fusion = f32[512,512]{0,1:T(8,128)} fusion(f32[1024,512]{0,1:T(8,128)S(1)} %bitcast_subtract_fusion.1, f32[1024,512]{1,0:T(8,128)} %collective-permute-done.7), kind=kOutput, calls=%fused_computation.4 | convolution fusion | flops 1610612736 | bytes 5242880 | tf_op jit(solution)/shard_map/dot_general | solution.py:88
  337.3 21.3 %collective-permute-done.6 = f32[512,512]{1,0:T(8,128)} collective-permute-done((f32[512,512]{1,0:T(8,128)S(1)}, f32[512,512]{1,0:T(8,128)}, u32[]{:S(2)}, u32[]{:S(2)}) %collective-permute-start.6) | collective-permute-done | bytes 1048608 | tf_op jit(solution)/shard_map/ppermute | solution.py:18
  358.6 11.0 %reduce-scatter.11.cloned.1.call-done = f32[512,64]{0,1:T(8,128)} async-done(((f32[512,512]{0,1:T(8,128)}), f32[512,64]{0,1:T(8,128)}) %reduce-scatter.11.cloned.1.call-update) | async-done | bytes 131088 | tf_op jit(solution)/shard_map/reduce_scatter | solution.py:107
  369.5 3.0 fusion.5
  375.6 17.4 %all-gather.11.cloned.1.call-done = f32[512,512]{0,1:T(8,128)} async-done(((f32[512,64]{0,1:T(8,128)}), f32[512,512]{0,1:T(8,128)}) %all-gather.11.cloned.1.call-update) | async-done | bytes 1048592 | tf_op jit(solution)/shard_map/all_gather | solution.py:109
  401.3 16.6 %collective-permute-done.5 = f32[512,512]{0,1:T(8,128)} collective-permute-done((f32[512,512]{0,1:T(8,128)}, f32[512,512]{0,1:T(8,128)}, u32[]{:S(2)}, u32[]{:S(2)}) %collective-permute-start.5) | collective-permute-done | bytes 1048608 | tf_op jit(solution)/shard_map/ppermute | solution.py:18
  421.1 4.8 %bitcast_subtract_fusion = f32[1024,512]{0,1:T(8,128)} fusion(f32[1024,512]{0,1:T(8,128)S(1)} %copy-done.2, f32[512,512]{0,1:T(8,128)S(1)} %copy-done.8, f32[1024,512]{1,0:T(8,128)} %collective-permute-done.7), kind=kOutput, calls=%fused_computation | convolution fusion | flops 1611137024 | bytes 7340032 | tf_op jit(solution)/shard_map/dot_general | solution.py:110
  (60 shorter events, 29.4 us)
Async XLA Ops:
  7.2 7.0 %copy-start = (f32[1024,512]{1,0:T(8,128)S(1)}, f32[1024,512]{1,0:T(8,128)}, u32[]{:S(2)}) copy-start(f32[1024,512]{1,0:T(8,128)} %param.2) | copy-start | bytes 6291460
  7.2 69.1 %all-reduce.2.cloned.1.call-start = ((), (), s32[]{:S(2)}) async-start(), calls=%async_computation.4 | async-start | bytes 2097152 | tf_op jit(solution)/shard_map/psum | solution.py:99
  14.1 96.3 %reduce-scatter.13.cloned.1.call-start = ((), (), s32[]{:S(2)}) async-start(), calls=%async_computation.12 | async-start | bytes 1179648
  18.6 115.3 %all-gather.5.cloned.1.call-start = ((), (), s32[]{:S(2)}) async-start(), calls=%async_computation.5 | async-start | bytes 1179648 | tf_op jit(solution)/shard_map/all_gather | solution.py:109
  113.4 84.0 %reduce-scatter.7.cloned.1.call-start = ((), (), s32[]{:S(2)}) async-start(), calls=%async_computation.6 | async-start | bytes 1179648 | tf_op jit(solution)/shard_map/reduce_scatter | solution.py:107
  113.4 44.3 %collective-permute-start.1 = (f32[1024,512]{1,0:T(8,128)S(1)}, f32[1024,512]{1,0:T(8,128)}, u32[]{:S(2)}, u32[]{:S(2)}) collective-permute-start(f32[1024,512]{1,0:T(8,128)S(1)} %copy-done), channel_id=1, source_target_pairs={{1,0},{2,1},{3,2},{0,3},{5,4},{6,5},{7,6},{4,7},{9,8},{10,9},{11,1... | collective-permute-start | bytes 6291464 | tf_op jit(solution)/shard_map/ppermute | solution.py:18
  137.8 19.9 %copy-start.4 = (f32[1024,512]{0,1:T(8,128)}, f32[1024,512]{0,1:T(8,128)S(1)}, u32[]{:S(2)}) copy-start(f32[1024,512]{0,1:T(8,128)S(1)} %bitcast_subtract_fusion.3) | copy-start | bytes 6291460
  137.8 24.4 %copy-start.9 = (f32[512,512]{1,0:T(8,128)S(1)}, f32[512,512]{1,0:T(8,128)}, u32[]{:S(2)}) copy-start(f32[512,512]{1,0:T(8,128)} %shard_map.41) | copy-start | bytes 3145732
  162.1 59.0 %all-gather.7.cloned.1.call-start = ((), (), s32[]{:S(2)}) async-start(), calls=%async_computation.7 | async-start | bytes 1179648 | tf_op jit(solution)/shard_map/all_gather | solution.py:109
  162.2 21.9 %collective-permute-start = (f32[512,512]{1,0:T(8,128)S(1)}, f32[512,512]{1,0:T(8,128)}, u32[]{:S(2)}, u32[]{:S(2)}) collective-permute-start(f32[512,512]{1,0:T(8,128)S(1)} %copy-done.9), channel_id=1, source_target_pairs={{1,0},{2,1},{3,2},{0,3},{5,4},{6,5},{7,6},{4,7},{9,8},{10,9},{11,1... | collective-permute-start | bytes 3145736 | tf_op jit(solution)/shard_map/ppermute | solution.py:18
  200.4 82.6 %reduce-scatter.9.cloned.1.call-start = ((), (), s32[]{:S(2)}) async-start(), calls=%async_computation.8 | async-start | bytes 1179648 | tf_op jit(solution)/shard_map/reduce_scatter | solution.py:107
  200.4 44.3 %collective-permute-start.4 = (f32[1024,512]{1,0:T(8,128)S(1)}, f32[1024,512]{1,0:T(8,128)}, u32[]{:S(2)}, u32[]{:S(2)}) collective-permute-start(f32[1024,512]{1,0:T(8,128)S(1)} %copy-done), channel_id=1, source_target_pairs={{2,0},{3,1},{0,2},{1,3},{6,4},{7,5},{4,6},{5,7},{10,8},{11,9},{8,1... | collective-permute-start | bytes 6291464 | tf_op jit(solution)/shard_map/ppermute | solution.py:18
  225.6 19.1 %copy-start.3 = (f32[1024,512]{0,1:T(8,128)}, f32[1024,512]{0,1:T(8,128)S(1)}, u32[]{:S(2)}) copy-start(f32[1024,512]{0,1:T(8,128)S(1)} %bitcast_subtract_fusion.2) | copy-start | bytes 6291460
  249.2 57.5 %all-gather.9.cloned.1.call-start = ((), (), s32[]{:S(2)}) async-start(), calls=%async_computation.9 | async-start | bytes 1179648 | tf_op jit(solution)/shard_map/all_gather | solution.py:109
  249.2 21.1 %collective-permute-start.3 = (f32[512,512]{1,0:T(8,128)S(1)}, f32[512,512]{1,0:T(8,128)}, u32[]{:S(2)}, u32[]{:S(2)}) collective-permute-start(f32[512,512]{1,0:T(8,128)S(1)} %copy-done.9), channel_id=1, source_target_pairs={{2,0},{3,1},{0,2},{1,3},{6,4},{7,5},{4,6},{5,7},{10,8},{11,9},{8,1... | collective-permute-start | bytes 3145736 | tf_op jit(solution)/shard_map/ppermute | solution.py:18
  286.0 83.5 %reduce-scatter.11.cloned.1.call-start = ((), (), s32[]{:S(2)}) async-start(), calls=%async_computation.10 | async-start | bytes 1179648 | tf_op jit(solution)/shard_map/reduce_scatter | solution.py:107
  286.1 45.7 %collective-permute-start.7 = (f32[1024,512]{1,0:T(8,128)S(1)}, f32[1024,512]{1,0:T(8,128)}, u32[]{:S(2)}, u32[]{:S(2)}) collective-permute-start(f32[1024,512]{1,0:T(8,128)S(1)} %copy-done), channel_id=1, source_target_pairs={{3,0},{0,1},{1,2},{2,3},{7,4},{4,5},{5,6},{6,7},{11,8},{8,9},{9,10... | collective-permute-start | bytes 6291464 | tf_op jit(solution)/shard_map/ppermute | solution.py:18
  311.2 20.6 %copy-start.1 = (f32[1024,512]{0,1:T(8,128)}, f32[1024,512]{0,1:T(8,128)S(1)}, u32[]{:S(2)}) copy-start(f32[1024,512]{0,1:T(8,128)S(1)} %bitcast_subtract_fusion.1) | copy-start | bytes 6291460
  331.8 4.6 %copy-start.10 = (f32[512,512]{1,0:T(8,128)S(1)}, f32[512,512]{1,0:T(8,128)}, u32[]{:S(2)}) copy-start(f32[512,512]{1,0:T(8,128)} %shard_map.41) | copy-start | bytes 3145732
  336.3 36.3 %copy-start.7 = (f32[512,512]{0,1:T(8,128)S(1)}, f32[512,512]{0,1:T(8,128)}, u32[]{:S(2)}) copy-start(f32[512,512]{0,1:T(8,128)} %all-gather.7.cloned.1.call-done) | copy-start | bytes 3145732
  336.3 59.5 %copy-start.5 = (f32[512,512]{0,1:T(8,128)S(1)}, f32[512,512]{0,1:T(8,128)}, u32[]{:S(2)}) copy-start(f32[512,512]{0,1:T(8,128)} %all-gather.5.cloned.1.call-done) | copy-start | bytes 3145732
  336.3 56.7 %all-gather.11.cloned.1.call-start = ((), (), s32[]{:S(2)}) async-start(), calls=%async_computation.11 | async-start | bytes 1179648 | tf_op jit(solution)/shard_map/all_gather | solution.py:109
  336.4 22.2 %collective-permute-start.6 = (f32[512,512]{1,0:T(8,128)S(1)}, f32[512,512]{1,0:T(8,128)}, u32[]{:S(2)}, u32[]{:S(2)}) collective-permute-start(f32[512,512]{1,0:T(8,128)S(1)} %copy-done.10), channel_id=1, source_target_pairs={{3,0},{0,1},{1,2},{2,3},{7,4},{4,5},{5,6},{6,7},{11,8},{8,9},{9,10... | collective-permute-start | bytes 3145736 | tf_op jit(solution)/shard_map/ppermute | solution.py:18
  372.6 26.1 %collective-permute-start.2 = (f32[512,512]{0,1:T(8,128)S(1)}, f32[512,512]{0,1:T(8,128)}, u32[]{:S(2)}, u32[]{:S(2)}) collective-permute-start(f32[512,512]{0,1:T(8,128)S(1)} %copy-done.7), channel_id=1, source_target_pairs={{3,0},{0,1},{1,2},{2,3},{7,4},{4,5},{5,6},{6,7},{11,8},{8,9},{9,10... | collective-permute-start | bytes 3145736 | tf_op jit(solution)/shard_map/ppermute | solution.py:18
  374.0 43.9 %collective-permute-start.5 = (f32[512,512]{0,1:T(8,128)}, f32[512,512]{0,1:T(8,128)}, u32[]{:S(2)}, u32[]{:S(2)}) collective-permute-start(f32[512,512]{0,1:T(8,128)} %all-gather.9.cloned.1.call-done), channel_id=1, source_target_pairs={{2,0},{3,1},{0,2},{1,3},{6,4},{7,5},{4,6},{5,7},{10,8},{11,9},{8,1... | collective-permute-start | bytes 3145736 | tf_op jit(solution)/shard_map/ppermute | solution.py:18
  393.0 35.7 %collective-permute-start.8 = (f32[512,512]{0,1:T(8,128)}, f32[512,512]{0,1:T(8,128)}, u32[]{:S(2)}, u32[]{:S(2)}) collective-permute-start(f32[512,512]{0,1:T(8,128)} %all-gather.11.cloned.1.call-done), channel_id=1, source_target_pairs={{1,0},{2,1},{3,2},{0,3},{5,4},{6,5},{7,6},{4,7},{9,8},{10,9},{11,1... | collective-permute-start | bytes 3145736 | tf_op jit(solution)/shard_map/ppermute | solution.py:18
  396.7 2.0 copy-start.6
  401.3 19.2 %copy-start.2 = (f32[1024,512]{0,1:T(8,128)S(1)}, f32[1024,512]{0,1:T(8,128)}, u32[]{:S(2)}) copy-start(f32[1024,512]{0,1:T(8,128)} %copy-done.1) | copy-start | bytes 6291460
  419.5 1.6 copy-start.8
Sparse Core Ops, SparseCore 0:
  14.2 62.0 all-reduce.1
  78.5 31.7 reduce-scatter.12
  113.5 20.3 all-gather.4
  162.3 35.0 reduce-scatter.6
  200.5 20.5 all-gather.6
  249.3 33.6 reduce-scatter.8
  286.1 20.4 all-gather.8
  336.4 33.0 reduce-scatter.10
  372.7 20.2 all-gather.10

commit v2 on v1

--- a/solution.py
+++ b/solution.py
@@ -90,28 +90,240 @@
     )
 
 
+def split(x):
+    high = x.astype(jnp.bfloat16)
+    return high, (x - high.astype(jnp.float32)).astype(jnp.bfloat16)
+
+
+def dot3(a, b, contract):
+    dims = (contract, ((), ()))
+    mul = functools.partial(
+        lax.dot_general, dimension_numbers=dims, preferred_element_type=jnp.float32
+    )
+    return mul(a[0], b[0]) + (mul(a[0], b[1]) + mul(a[1], b[0]))
+
+
+def sweep_kernel(
+    nb, nrows, x_ref, t_ref, gram_ref, coef_ref, out_ref,
+    xbuf, xh, xl, rest, ginv, part, gpart, gpair, grs, gfull, pairb, rsb, full, cbuf,
+    fsem, psem, rsem, asem, wsem, isem, jsem, csem, dsem,
+):
+    r, g = lax.axis_index("rows"), lax.axis_index("feat")
+    nz = nrows // 2
+    z, c = r // 2, r % 2
+    width, tg = x_ref.shape[1], t_ref.shape[1]
+    mate = (r + 1 - 2 * c, g)
+
+    def along(d):
+        return (((z + d) % nz) * 2 + c, g)
+
+    def owner_of(s):
+        return (r, (g + s) % nb)
+
+    def remote(src, dst, sems, at, device):
+        return pltpu.make_async_remote_copy(
+            src_ref=src, dst_ref=dst, send_sem=sems.at[(0,) + at], recv_sem=sems.at[(1,) + at],
+            device_id=device, device_id_type=pl.DeviceIdType.MESH,
+        )
+
+    def rows_of(start, size):
+        return pl.ds(pl.multiple_of(start, 8), size)
+
+    barrier = pltpu.get_barrier_semaphore()
+    peers = [mate] + [along(d) for d in range(1, nz)] + [owner_of(s) for s in range(1, nb)]
+    for peer in peers:
+        pl.semaphore_signal(barrier, inc=1, device_id=peer, device_id_type=pl.DeviceIdType.MESH)
+    pl.semaphore_wait(barrier, len(peers))
+
+    def block_copy(s):
+        return remote(x_ref, xbuf.at[s - 1], fsem, (s - 1,), owner_of(nb - s))
+
+    def all_reduce(k, n, src, pair_buf, rs_buf, dst, second, finish):
+        half, size = n // 2, n // 2 // nz
+        swap = remote(src.at[rows_of((1 - c) * half, half)], pair_buf, psem, (k,), mate)
+        swap.start()
+        second()
+        swap.wait_recv()
+        sends = [swap]
+        for d in range(1, nz):
+            slot = ((z + d) % nz) * size
+            at = rows_of(c * half + slot, size)
+            src[at, :] += pair_buf[rows_of(slot, size), :]
+            copy = remote(src.at[at], rs_buf.at[d - 1], rsem, (k, d - 1), along(d))
+            copy.start()
+            sends.append(copy)
+        total = src[rows_of(c * half + z * size, size), :] + pair_buf[rows_of(z * size, size), :]
+        for d in range(1, nz):
+            sends[d].wait_recv()
+            total = total + rs_buf[d - 1]
+        own = dst.at[rows_of(c * half + z * size, size)]
+        own[...] = finish(total)
+        spread = []
+        for d in range(1, nz):
+            copy = remote(own, own, asem, (k, d - 1), along(d))
+            copy.start()
+            spread.append(copy)
+        relay = [remote(own, own, wsem, (k, 0), mate)]
+        relay[0].start()
+        for d in range(1, nz):
+            spread[d - 1].wait_recv()
+            piece = dst.at[rows_of(c * half + ((z - d + nz) % nz) * size, size)]
+            relay.append(remote(piece, piece, wsem, (k, d), mate))
+            relay[d].start()
+        for copy in relay:
+            copy.wait_recv()
+        for copy in sends + spread + relay:
+            copy.wait_send()
+
+    def tiles(count, body):
+        lax.fori_loop(0, count, lambda i, _: (body(i), 0)[1], 0)
+
+    gpart[...] = gram_ref[...]
+    tile = 128
+
+    def turn(i):
+        at = pl.ds(pl.multiple_of(i * tile, tile), tile)
+        rest[at, :] = t_ref[:, at].T
+
+    def start_blocks():
+        for s in range(1, nb):
+            block_copy(s).start()
+        tiles(tg // tile, turn)
+
+    all_reduce(0, width, gpart, gpair, grs, gfull, start_blocks, lambda v: v)
+    invert_kernel(min(128, width), gfull, ginv.at[0])
+
+    wh = width // 2
+    mine = pl.ds(pl.multiple_of(c * wh, wh), wh)
+
+    def inverse_copy(s):
+        return remote(
+            ginv.at[0, mine], ginv.at[s, mine], isem, (s - 1,), owner_of(nb - s)
+        )
+
+    def inverse_relay(s):
+        return remote(ginv.at[s, mine], ginv.at[s, mine], jsem, (s - 1,), mate)
+
+    for s in range(1, nb):
+        inverse_copy(s).start()
+
+    def columns(group):
+        return pl.ds(pl.multiple_of(group * tg, tg), tg)
+
+    def coef_copy(s):
+        return remote(
+            cbuf.at[s - 1], coef_ref.at[mine, columns(g)], csem, (s - 1,), owner_of(s)
+        )
+
+    def coef_relay(s):
+        piece = coef_ref.at[mine, columns((g - s + nb) % nb)]
+        return remote(piece, piece, dsem, (s - 1,), mate)
+
+    for s in range(nb):
+        if s:
+            inverse_copy(s).wait_recv()
+            inverse_relay(s).start()
+            block_copy(s).wait_recv()
+        block = xbuf.at[s - 1] if s else x_ref
+
+        def cut(i):
+            at = pl.ds(pl.multiple_of(i * tile, tile), tile)
+            xh[at, :], xl[at, :] = split(block[at, :])
+
+        tiles(block.shape[0] // tile, cut)
+
+        def product(side):
+            def body(i):
+                at = rows_of(side * (tg // 2) + i * (tg // 4), tg // 4)
+                part[at, :] = dot3(split(rest[at, :]), (xh[...], xl[...]), ((1,), (0,)))
+
+            tiles(2, body)
+
+        product(1 - c)
+
+        def solve(total):
+            if s:
+                inverse_relay(s).wait_recv()
+            return jnp.dot(total, ginv[s], precision=HI, preferred_element_type=jnp.float32)
+
+        all_reduce(
+            s + 1, tg, part, pairb.at[s], rsb.at[s], full.at[s], lambda: product(c), solve
+        )
+        step = full.at[s]
+        if s:
+            cbuf[s - 1] = step[:, mine].T
+            coef_copy(s).start()
+        else:
+            coef_ref[:, columns(g)] = step[...].T
+        if s > 1:
+            coef_copy(s - 1).wait_recv()
+            coef_relay(s - 1).start()
+
+        def update(i):
+            at = rows_of(i * (tg // 4), tg // 4)
+            rest[at, :] -= dot3(split(step[at, :]), (xh[...], xl[...]), ((1,), (1,)))
+
+        tiles(4, update)
+
+    def turn_back(i):
+        at = pl.ds(pl.multiple_of(i * tile, tile), tile)
+        out_ref[:, at] = rest[at, :].T
+
+    tiles(tg // tile, turn_back)
+    if nb > 1:
+        coef_copy(nb - 1).wait_recv()
+        coef_relay(nb - 1).start()
+    for s in range(1, nb):
+        coef_relay(s).wait_recv()
+    for s in range(1, nb):
+        for copy in (block_copy, inverse_copy, inverse_relay, coef_copy, coef_relay):
+            copy(s).wait_send()
+
+
 def gathered(features, targets):
-    high = lax.Precision.HIGH
-    nblocks = lax.axis_size("feat")
-    owner = lax.axis_index("feat")
-    width = features.shape[1]
-    group_width = targets.shape[1]
-    gram = lax.psum(tmul(features, features, HI), "rows")
-    blocks = [features] + [shifted(features, "feat", -s) for s in range(1, nblocks)]
-    inverse = invert(gram)
-    inverses = [inverse] + [shifted(inverse, "feat", -s) for s in range(1, nblocks)]
-    res = targets
-    coef = jnp.zeros((width, group_width * nblocks), jnp.float32)
-    for s in range(nblocks):
-        product = tmul(blocks[s], res, high)
-        share = lax.psum_scatter(product, "rows", scatter_dimension=1, tiled=True)
-        part = jnp.dot(inverses[s], share, precision=HI, preferred_element_type=jnp.float32)
-        step = lax.all_gather(part, "rows", axis=1, tiled=True)
-        res = res - jnp.dot(blocks[s], step, precision=high, preferred_element_type=jnp.float32)
-        back = shifted(step, "feat", s) if s else step
-        start = ((owner - s) % nblocks) * group_width
-        coef = lax.dynamic_update_slice_in_dim(coef, back, start, 1)
-    return (coef, res)
+    nb, nrows = lax.axis_size("feat"), lax.axis_size("rows")
+    height, width = features.shape
+    tg = targets.shape[1]
+    nz = nrows // 2
+    f32 = jnp.float32
+    gram = tmul(features, features, HI)
+    vmem = pl.BlockSpec(memory_space=pltpu.VMEM)
+    dma = pltpu.SemaphoreType.DMA
+    return pl.pallas_call(
+        functools.partial(sweep_kernel, nb, nrows),
+        out_shape=(
+            jax.ShapeDtypeStruct((width, tg * nb), f32),
+            jax.ShapeDtypeStruct((height, tg), f32),
+        ),
+        in_specs=[vmem] * 3,
+        out_specs=(vmem, vmem),
+        scratch_shapes=[
+            pltpu.VMEM((nb - 1, height, width), f32),
+            pltpu.VMEM((height, width), jnp.bfloat16),
+            pltpu.VMEM((height, width), jnp.bfloat16),
+            pltpu.VMEM((tg, height), f32),
+            pltpu.VMEM((nb, width, width), f32),
+            pltpu.VMEM((tg, width), f32),
+            pltpu.VMEM((width, width), f32),
+            pltpu.VMEM((width // 2, width), f32),
+            pltpu.VMEM((nz - 1, width // nrows, width), f32),
+            pltpu.VMEM((width, width), f32),
+            pltpu.VMEM((nb, tg // 2, width), f32),
+            pltpu.VMEM((nb, nz - 1, tg // nrows, width), f32),
+            pltpu.VMEM((nb, tg, width), f32),
+            pltpu.VMEM((nb - 1, width // 2, tg), f32),
+            dma((2, nb - 1)),
+            dma((2, nb + 1)),
+            dma((2, nb + 1, nz - 1)),
+            dma((2, nb + 1, nz - 1)),
+            dma((2, nb + 1, nz)),
+            dma((2, nb - 1)),
+            dma((2, nb - 1)),
+            dma((2, nb - 1)),
+            dma((2, nb - 1)),
+        ],
+        compiler_params=pltpu.CompilerParams(collective_id=0, has_side_effects=True),
+    )(features, targets, gram)
 
 
 def general(features, targets):
@@ -141,7 +353,12 @@
 
 def on_device(features, targets):
     nblocks = lax.axis_size("feat")
-    if SWEEPS == 1 and nblocks * features.size * 4 <= GATHER_BYTES:
+    nrows = lax.axis_size("rows")
+    width, group_width = features.shape[1], targets.shape[1]
+    fits = nblocks > 1 and nblocks * features.size * 4 <= GATHER_BYTES
+    whole = nrows % 2 == 0 and nrows > 2 and features.shape[0] % 128 == 0
+    even = width % max(256, 8 * nrows) == 0 and group_width % max(128, 8 * nrows) == 0
+    if SWEEPS == 1 and fits and whole and even:
         return gathered(features, targets)
     return general(features, targets)
 

time: 438 us -> 241 us (0.55)
  waiting for transfers between devices: 311 us -> 0 us
  Pallas kernels: 22.3 us -> 227 us
  matrix products: 54.4 us -> 6.68 us
  starting transfers between devices: 18.6 us -> 0 us
  between operations: 14 us -> 0.65 us
  local copies, waits for them, and re-layouts: 17.1 us -> 6.17 us
    pallas_call x1, Pallas kernels: 22.3 us -> 227 us  [gathered(): pl.pallas_call(functools.partial(sweep_kernel, nb, nrows), out_shape=(jax...]
    ppermute x9 -> x0, waiting for transfers between devices: 135 us -> none  [shifted(): return lax.ppermute(block, axis, route)]
    all_gather x4 -> x0, waiting for transfers between devices: 69.9 us -> none  [gathered(): step = lax.all_gather(part, 'rows', axis=1, tiled=True)]
    psum x1 -> x0, waiting for transfers between devices: 57.6 us -> none  [gathered(): gram = lax.psum(tmul(features, features, HI), 'rows')]
    reduce_scatter x3 -> x0, waiting for transfers between devices: 36.8 us -> none  [gathered(): share = lax.psum_scatter(product, 'rows', scatter_dimension=1, tiled=True)]
    dot_general x8 -> x0, matrix products: 29.8 us -> none  [the longest x4 17.7 us: gathered(): jnp.dot(blocks[s], step, precision=high, preferred_element_type=jnp.float32)]
    ppermute x9 -> x0, starting transfers between devices: 18.2 us -> none  [shifted(): return lax.ppermute(block, axis, route)]
    dot_general x4 -> x1, matrix products: 20.2 us -> 6.68 us  [tmul(): lax.dot_general(a, b, (((0,), (0,)), ((), ())), precision=precision, pref...]
  transfers between devices with their start and end apart: 18 -> 0, of which waited for: 16 -> 0; matrix products, arithmetic and copies ran while one was open for 8% -> 0% of each run, Pallas kernels for 5% -> 0%
where the time goes in v2:
time: 241 us
  Pallas kernels  227 us (94%)
  matrix products  6.68 us (3%)
  local copies, waits for them, and re-layouts  6.17 us (3%)
    pallas_call x1, Pallas kernels, gathered(): pl.pallas_call(functools.partial(sweep_kernel, nb, nrows), out_shape=(jax...  227 us
    dot_general x1, matrix products, tmul(): lax.dot_general(a, b, (((0,), (0,)), ((), ())), precision=precision, pref...  6.68 us
    unnamed x4, local copies, waits for them, and re-layouts  6.17 us

profile of v2, /device:TPU:0, one launch (start us, length us, event | category | flops | bytes accessed | tf_op | source)
XLA Modules:
  0.0 240.8 jit_solution(16469256942664835385)
XLA Ops:
  0.6 6.7 %fusion.gram_ref = f32[512,512]{1,0:T(8,128)} fusion(f32[1024,512]{1,0:T(8,128)} %x_ref.1), kind=kOutput, calls=%fused_computation | convolution fusion | flops 3221225472 | bytes 3145728 | tf_op jit(solution)/shard_map/dot_general | solution.py:88
  7.3 227.3 %shard_map.41 = (f32[512,2048]{1,0:T(8,128)}, f32[1024,512]{1,0:T(8,128)}) custom-call(f32[1024,512]{1,0:T(8,128)} %x_ref.1, f32[1024,512]{1,0:T(8,128)} %t_ref.1, f32[512,512]{1,0:T(8,128)} %fusion.gram_ref), custom_call_target="tpu_custom_call" | custom-call | tf_op jit(solution)/shard_map/pallas_call | solution.py:292
  234.6 0.0 copy-start
  234.7 4.8 %copy.6 = f32[512,2048]{1,0:T(8,128)} copy(f32[512,2048]{1,0:T(8,128)} %get-tuple-element.4) | data formatting | bytes 8388608
  239.5 0.0 copy-done
  239.5 1.3 copy.7
Async XLA Ops:
  234.6 4.9 %copy-start = (f32[1024,512]{1,0:T(8,128)S(1)}, f32[1024,512]{1,0:T(8,128)}, u32[]{:S(2)}) copy-start(f32[1024,512]{1,0:T(8,128)} %get-tuple-element.5) | copy-start | bytes 6291460

commit v3 on v1

--- a/solution.py
+++ b/solution.py
@@ -90,28 +90,346 @@
     )
 
 
+def split(x):
+    high = x.astype(jnp.bfloat16)
+    return high, (x - high.astype(jnp.float32)).astype(jnp.bfloat16)
+
+
+def dot3(a, b, contract):
+    dims = (contract, ((), ()))
+    mul = functools.partial(
+        lax.dot_general, dimension_numbers=dims, preferred_element_type=jnp.float32
+    )
+    return mul(a[0], b[0]) + (mul(a[0], b[1]) + mul(a[1], b[0]))
+
+
+class RowSum:
+    def __init__(self, net, k, n, src, pair_buf, rs_buf, dst):
+        self.net, self.k, self.src, self.dst = net, k, src, dst
+        self.pair_buf, self.rs_buf = pair_buf, rs_buf
+        self.half, self.size = n // 2, n // 2 // net.nz
+
+    def slot(self, d):
+        net = self.net
+        return rows_of(net.c * self.half + ((net.z + d) % net.nz) * self.size, self.size)
+
+    def pair_slot(self, d):
+        return rows_of(((self.net.z + d) % self.net.nz) * self.size, self.size)
+
+    def swap(self):
+        net = self.net
+        away = self.src.at[rows_of((1 - net.c) * self.half, self.half)]
+        self.sends = [net.copy(away, self.pair_buf, net.psem, (self.k,), net.mate)]
+        self.sends[0].start()
+
+    def scatter(self):
+        net = self.net
+        self.sends[0].wait_recv()
+        for d in range(1, net.nz):
+            at = self.slot(d)
+            self.src[at, :] += self.pair_buf[self.pair_slot(d), :]
+            copy = net.copy(
+                self.src.at[at], self.rs_buf.at[d - 1], net.rsem, (self.k, d - 1), net.along(d)
+            )
+            copy.start()
+            self.sends.append(copy)
+
+    def finish(self, apply):
+        net = self.net
+        total = self.src[self.slot(0), :] + self.pair_buf[self.pair_slot(0), :]
+        for d in range(1, net.nz):
+            self.sends[d].wait_recv()
+            total = total + self.rs_buf[d - 1]
+        own = self.dst.at[self.slot(0)]
+        own[...] = apply(total)
+        self.spread = []
+        for d in range(1, net.nz):
+            copy = net.copy(own, own, net.asem, (self.k, d - 1), net.along(d))
+            copy.start()
+            self.spread.append(copy)
+        self.relay = [net.copy(own, own, net.wsem, (self.k, 0), net.mate)]
+        self.relay[0].start()
+
+    def collect(self):
+        net = self.net
+        for d in range(1, net.nz):
+            self.spread[d - 1].wait_recv()
+            piece = self.dst.at[self.slot(net.nz - d)]
+            self.relay.append(net.copy(piece, piece, net.wsem, (self.k, d), net.mate))
+            self.relay[d].start()
+        for copy in self.relay:
+            copy.wait_recv()
+        for copy in self.sends + self.spread + self.relay:
+            copy.wait_send()
+
+
+class Net:
+    def __init__(self, nb, nrows, psem, rsem, asem, wsem):
+        self.nb, self.nz = nb, nrows // 2
+        self.r, self.g = lax.axis_index("rows"), lax.axis_index("feat")
+        self.z, self.c = self.r // 2, self.r % 2
+        self.mate = (self.r + 1 - 2 * self.c, self.g)
+        self.psem, self.rsem, self.asem, self.wsem = psem, rsem, asem, wsem
+
+    def along(self, d):
+        return (((self.z + d) % self.nz) * 2 + self.c, self.g)
+
+    def owner_of(self, s):
+        return (self.r, (self.g + s) % self.nb)
+
+    def copy(self, src, dst, sems, at, device):
+        return pltpu.make_async_remote_copy(
+            src_ref=src, dst_ref=dst, send_sem=sems.at[(0,) + at], recv_sem=sems.at[(1,) + at],
+            device_id=device, device_id_type=pl.DeviceIdType.MESH,
+        )
+
+    def greet(self):
+        barrier = pltpu.get_barrier_semaphore()
+        peers = [self.mate] + [self.along(d) for d in range(1, self.nz)]
+        peers += [self.owner_of(s) for s in range(1, self.nb)]
+        for peer in peers:
+            pl.semaphore_signal(
+                barrier, inc=1, device_id=peer, device_id_type=pl.DeviceIdType.MESH
+            )
+        pl.semaphore_wait(barrier, len(peers))
+
+
+def rows_of(start, size):
+    return pl.ds(pl.multiple_of(start, 8), size)
+
+
+def tiles(count, body):
+    lax.fori_loop(0, count, lambda i, _: (body(i), 0)[1], 0)
+
+
+TILE = 128
+CHUNKS = 2
+
+
+def sweep_kernel(
+    nb, nrows, x_ref, t_ref, coef_ref, out_ref,
+    xbuf, xh, xl, rest, ginv, part, xt, gpart, gpair, grs, gsum, gfull, pairb, rsb, full, cbuf,
+    fsem, psem, rsem, asem, wsem, isem, jsem, csem, dsem,
+):
+    net = Net(nb, nrows, psem, rsem, asem, wsem)
+    c, g = net.c, net.g
+    height, width = x_ref.shape
+    tg = t_ref.shape[1]
+    chunk = tg // CHUNKS
+    net.greet()
+
+    def block_copy(s):
+        return net.copy(x_ref, xbuf.at[s - 1], fsem, (s - 1,), net.owner_of(nb - s))
+
+    block_copy(1).start()
+
+    m = width // TILE
+    pairs = [(i, j) for i in range(m) for j in range(i + 1)]
+    for i in range(m):
+        xt[...] = x_ref[:, i * TILE : (i + 1) * TILE].T
+        low = jnp.dot(
+            xt[...], x_ref[:, : (i + 1) * TILE], precision=HI, preferred_element_type=jnp.float32
+        )
+        for j in range(i + 1):
+            at = pairs.index((i, j)) * TILE
+            gpart[at : at + TILE, :] = low[:, j * TILE : (j + 1) * TILE]
+    gram = RowSum(net, 0, len(pairs) * TILE, gpart, gpair, grs, gsum)
+    gram.swap()
+
+    def turn(i):
+        at = pl.ds(pl.multiple_of(i * TILE, TILE), TILE)
+        rest[at, :] = t_ref[:, at].T
+
+    def cut(s):
+        block = xbuf.at[s - 1] if s else x_ref
+
+        def body(i):
+            at = pl.ds(pl.multiple_of(i * TILE, TILE), TILE)
+            xh[s % 2, at, :], xl[s % 2, at, :] = split(block[at, :])
+
+        tiles(height // TILE, body)
+
+    sums = [
+        [
+            RowSum(
+                net, 1 + s * CHUNKS + p, chunk, part.at[p], pairb.at[s, p], rsb.at[s, p],
+                full.at[s, p],
+            )
+            for p in range(CHUNKS)
+        ]
+        for s in range(nb)
+    ]
+
+    def product(s, p, side):
+        size = chunk // 2
+        res = split(rest[rows_of(p * chunk + side * size, size), :])
+        part[p, rows_of(side * size, size), :] = dot3(
+            res, (xh[s % 2], xl[s % 2]), ((1,), (0,))
+        )
+
+    def update(s, p):
+        def body(i):
+            size = chunk // 2
+            at = rows_of(i * size, size)
+            step = split(full[s, p, at, :])
+            rest[rows_of(p * chunk + i * size, size), :] -= dot3(
+                step, (xh[s % 2], xl[s % 2]), ((1,), (1,))
+            )
+
+        tiles(2, body)
+
+    gram.scatter()
+    tiles(tg // TILE, turn)
+    cut(0)
+    gram.finish(lambda v: v)
+    for p in range(CHUNKS):
+        product(0, p, 1 - c)
+        product(0, p, c)
+    gram.collect()
+    if nb > 2:
+        block_copy(2).start()
+    for p in range(CHUNKS):
+        sums[0][p].swap()
+    for p in range(CHUNKS):
+        sums[0][p].scatter()
+    for at, (i, j) in enumerate(pairs):
+        tile = gsum[at * TILE : (at + 1) * TILE, :]
+        gfull[i * TILE : (i + 1) * TILE, j * TILE : (j + 1) * TILE] = tile
+        if i != j:
+            gfull[j * TILE : (j + 1) * TILE, i * TILE : (i + 1) * TILE] = tile.T
+    invert_kernel(TILE, gfull, ginv.at[0])
+
+    wh = width // 2
+    mine = pl.ds(pl.multiple_of(c * wh, wh), wh)
+
+    def inverse_copy(s):
+        return net.copy(
+            ginv.at[0, mine], ginv.at[s, mine], isem, (s - 1,), net.owner_of(nb - s)
+        )
+
+    def inverse_relay(s):
+        return net.copy(ginv.at[s, mine], ginv.at[s, mine], jsem, (s - 1,), net.mate)
+
+    for s in range(1, nb):
+        inverse_copy(s).start()
+    for s in range(3, nb):
+        block_copy(s).start()
+
+    def columns(group, p):
+        return pl.ds(pl.multiple_of(group * tg + p * chunk, chunk), chunk)
+
+    def coef_copy(s, p):
+        return net.copy(
+            cbuf.at[s - 1, p], coef_ref.at[mine, columns(g, p)], csem, (s - 1, p),
+            net.owner_of(s),
+        )
+
+    def coef_relay(s, p):
+        piece = coef_ref.at[mine, columns((g - s + nb) % nb, p)]
+        return net.copy(piece, piece, dsem, (s - 1, p), net.mate)
+
+    def hand_over(s, p):
+        if s:
+            cbuf[s - 1, p] = full[s, p, :, mine].T
+            coef_copy(s, p).start()
+        else:
+            coef_ref[:, columns(g, p)] = full[s, p].T
+
+    for s in range(nb):
+        last = s + 1 == nb
+        if s:
+            inverse_relay(s).wait_recv()
+        for p in range(CHUNKS):
+            sums[s][p].finish(
+                lambda v: jnp.dot(v, ginv[s], precision=HI, preferred_element_type=jnp.float32)
+            )
+        if not last:
+            inverse_copy(s + 1).wait_recv()
+            inverse_relay(s + 1).start()
+            block_copy(s + 1).wait_recv()
+            cut(s + 1)
+        for p in range(CHUNKS):
+            sums[s][p].collect()
+            if last:
+                hand_over(s, p)
+            update(s, p)
+            if not last:
+                product(s + 1, p, 1 - c)
+                sums[s + 1][p].swap()
+                product(s + 1, p, c)
+                sums[s + 1][p].scatter()
+                hand_over(s, p)
+        if s > 1:
+            for p in range(CHUNKS):
+                coef_copy(s - 1, p).wait_recv()
+                coef_relay(s - 1, p).start()
+
+    def turn_back(i):
+        at = pl.ds(pl.multiple_of(i * TILE, TILE), TILE)
+        out_ref[:, at] = rest[at, :].T
+
+    tiles(tg // TILE, turn_back)
+    for p in range(CHUNKS):
+        coef_copy(nb - 1, p).wait_recv()
+        coef_relay(nb - 1, p).start()
+    for s in range(1, nb):
+        for copy in (block_copy, inverse_copy, inverse_relay):
+            copy(s).wait_send()
+        for p in range(CHUNKS):
+            coef_relay(s, p).wait_recv()
+            coef_copy(s, p).wait_send()
+            coef_relay(s, p).wait_send()
+
+
 def gathered(features, targets):
-    high = lax.Precision.HIGH
-    nblocks = lax.axis_size("feat")
-    owner = lax.axis_index("feat")
-    width = features.shape[1]
-    group_width = targets.shape[1]
-    gram = lax.psum(tmul(features, features, HI), "rows")
-    blocks = [features] + [shifted(features, "feat", -s) for s in range(1, nblocks)]
-    inverse = invert(gram)
-    inverses = [inverse] + [shifted(inverse, "feat", -s) for s in range(1, nblocks)]
-    res = targets
-    coef = jnp.zeros((width, group_width * nblocks), jnp.float32)
-    for s in range(nblocks):
-        product = tmul(blocks[s], res, high)
-        share = lax.psum_scatter(product, "rows", scatter_dimension=1, tiled=True)
-        part = jnp.dot(inverses[s], share, precision=HI, preferred_element_type=jnp.float32)
-        step = lax.all_gather(part, "rows", axis=1, tiled=True)
-        res = res - jnp.dot(blocks[s], step, precision=high, preferred_element_type=jnp.float32)
-        back = shifted(step, "feat", s) if s else step
-        start = ((owner - s) % nblocks) * group_width
-        coef = lax.dynamic_update_slice_in_dim(coef, back, start, 1)
-    return (coef, res)
+    nb, nrows = lax.axis_size("feat"), lax.axis_size("rows")
+    height, width = features.shape
+    tg = targets.shape[1]
+    nz = nrows // 2
+    chunk = tg // CHUNKS
+    m = width // TILE
+    packed = m * (m + 1) // 2 * TILE
+    f32 = jnp.float32
+    sums = 1 + nb * CHUNKS
+    vmem = pl.BlockSpec(memory_space=pltpu.VMEM)
+    dma = pltpu.SemaphoreType.DMA
+    return pl.pallas_call(
+        functools.partial(sweep_kernel, nb, nrows),
+        out_shape=(
+            jax.ShapeDtypeStruct((width, tg * nb), f32),
+            jax.ShapeDtypeStruct((height, tg), f32),
+        ),
+        in_specs=[vmem] * 2,
+        out_specs=(vmem, vmem),
+        scratch_shapes=[
+            pltpu.VMEM((nb - 1, height, width), f32),
+            pltpu.VMEM((2, height, width), jnp.bfloat16),
+            pltpu.VMEM((2, height, width), jnp.bfloat16),
+            pltpu.VMEM((tg, height), f32),
+            pltpu.VMEM((nb, width, width), f32),
+            pltpu.VMEM((CHUNKS, chunk, width), f32),
+            pltpu.VMEM((TILE, height), f32),
+            pltpu.VMEM((packed, TILE), f32),
+            pltpu.VMEM((packed // 2, TILE), f32),
+            pltpu.VMEM((nz - 1, packed // nrows, TILE), f32),
+            pltpu.VMEM((packed, TILE), f32),
+            pltpu.VMEM((width, width), f32),
+            pltpu.VMEM((nb, CHUNKS, chunk // 2, width), f32),
+            pltpu.VMEM((nb, CHUNKS, nz - 1, chunk // nrows, width), f32),
+            pltpu.VMEM((nb, CHUNKS, chunk, width), f32),
+            pltpu.VMEM((nb - 1, CHUNKS, width // 2, chunk), f32),
+            dma((2, nb - 1)),
+            dma((2, sums)),
+            dma((2, sums, nz - 1)),
+            dma((2, sums, nz - 1)),
+            dma((2, sums, nz)),
+            dma((2, nb - 1)),
+            dma((2, nb - 1)),
+            dma((2, nb - 1, CHUNKS)),
+            dma((2, nb - 1, CHUNKS)),
+        ],
+        compiler_params=pltpu.CompilerParams(collective_id=0, has_side_effects=True),
+    )(features, targets)
 
 
 def general(features, targets):
@@ -141,7 +459,14 @@
 
 def on_device(features, targets):
     nblocks = lax.axis_size("feat")
-    if SWEEPS == 1 and nblocks * features.size * 4 <= GATHER_BYTES:
+    nrows = lax.axis_size("rows")
+    width, group_width = features.shape[1], targets.shape[1]
+    fits = nblocks > 1 and nblocks * features.size * 4 <= GATHER_BYTES
+    whole = nrows % 2 == 0 and nrows > 2 and features.shape[0] % 128 == 0
+    packed = (width // TILE) * (width // TILE + 1) // 2 * TILE
+    even = width % (2 * TILE) == 0 and packed % (8 * nrows) == 0
+    even = even and group_width % (CHUNKS * max(TILE, 8 * nrows)) == 0
+    if SWEEPS == 1 and fits and whole and even:
         return gathered(features, targets)
     return general(features, targets)
 

time: 438 us -> 234 us (0.53)
  waiting for transfers between devices: 311 us -> 0 us
  Pallas kernels: 22.3 us -> 223 us
  matrix products: 54.4 us -> 0 us
  starting transfers between devices: 18.6 us -> 0 us
  between operations: 14 us -> 0.65 us
  local copies, waits for them, and re-layouts: 17.1 us -> 6.17 us
    pallas_call x1, Pallas kernels: 22.3 us -> 223 us  [gathered(): pl.pallas_call(functools.partial(sweep_kernel, nb, nrows), out_shape=(jax...]
    ppermute x9 -> x0, waiting for transfers between devices: 135 us -> none  [shifted(): return lax.ppermute(block, axis, route)]
    all_gather x4 -> x0, waiting for transfers between devices: 69.9 us -> none  [gathered(): step = lax.all_gather(part, 'rows', axis=1, tiled=True)]
    psum x1 -> x0, waiting for transfers between devices: 57.6 us -> none  [gathered(): gram = lax.psum(tmul(features, features, HI), 'rows')]
    dot_general x12 -> x0, matrix products: 50 us -> none  [the longest x4 20.2 us: tmul(): lax.dot_general(a, b, (((0,), (0,)), ((), ())), precision=precision, pref...]
    reduce_scatter x3 -> x0, waiting for transfers between devices: 36.8 us -> none  [gathered(): share = lax.psum_scatter(product, 'rows', scatter_dimension=1, tiled=True)]
    ppermute x9 -> x0, starting transfers between devices: 18.2 us -> none  [shifted(): return lax.ppermute(block, axis, route)]
    unnamed x10 -> x0, waiting for transfers between devices: 11.9 us -> none
  transfers between devices with their start and end apart: 18 -> 0, of which waited for: 16 -> 0; matrix products, arithmetic and copies ran while one was open for 8% -> 0% of each run, Pallas kernels for 5% -> 0%
where the time goes in v3:
time: 234 us; the launch traced here: 230 us
  Pallas kernels  223 us (95%)
  local copies, waits for them, and re-layouts  6.17 us (3%)
    pallas_call x1, Pallas kernels, gathered(): pl.pallas_call(functools.partial(sweep_kernel, nb, nrows), out_shape=(jax...  223 us
    unnamed x4, local copies, waits for them, and re-layouts  6.17 us

profile of v3, /device:TPU:0, one launch (start us, length us, event | category | flops | bytes accessed | tf_op | source)
XLA Modules:
  0.0 230.0 jit_solution(4953909073388494455)
XLA Ops:
  0.6 223.2 %shard_map.41 = (f32[512,2048]{1,0:T(8,128)}, f32[1024,512]{1,0:T(8,128)}) custom-call(f32[1024,512]{1,0:T(8,128)} %x_ref.1, f32[1024,512]{1,0:T(8,128)} %t_ref.1), custom_call_target="tpu_custom_call" | custom-call | tf_op jit(solution)/shard_map/pallas_call | solution.py:396
  223.8 0.0 copy-start
  223.9 4.8 %copy.6 = f32[512,2048]{1,0:T(8,128)} copy(f32[512,2048]{1,0:T(8,128)} %get-tuple-element.4) | data formatting | bytes 8388608
  228.7 0.0 copy-done
  228.7 1.3 copy.7
Async XLA Ops:
  223.8 4.9 %copy-start = (f32[1024,512]{1,0:T(8,128)S(1)}, f32[1024,512]{1,0:T(8,128)}, u32[]{:S(2)}) copy-start(f32[1024,512]{1,0:T(8,128)} %get-tuple-element.5) | copy-start | bytes 6291460

commit v4 on v3

--- a/solution.py
+++ b/solution.py
@@ -100,7 +100,9 @@
     mul = functools.partial(
         lax.dot_general, dimension_numbers=dims, preferred_element_type=jnp.float32
     )
-    return mul(a[0], b[0]) + (mul(a[0], b[1]) + mul(a[1], b[0]))
+    rows = a[0].shape[0]
+    both = mul(jnp.concatenate(a, axis=0), b[0])
+    return both[:rows] + (both[rows:] + mul(a[0], b[1]))
 
 
 class RowSum:
@@ -260,31 +262,20 @@
         for s in range(nb)
     ]
 
-    def product(s, p, side):
-        size = chunk // 2
-        res = split(rest[rows_of(p * chunk + side * size, size), :])
-        part[p, rows_of(side * size, size), :] = dot3(
-            res, (xh[s % 2], xl[s % 2]), ((1,), (0,))
-        )
+    def product(s, p):
+        res = split(rest[p * chunk : (p + 1) * chunk, :])
+        part[p] = dot3(res, (xh[s % 2], xl[s % 2]), ((1,), (0,)))
 
     def update(s, p):
-        def body(i):
-            size = chunk // 2
-            at = rows_of(i * size, size)
-            step = split(full[s, p, at, :])
-            rest[rows_of(p * chunk + i * size, size), :] -= dot3(
-                step, (xh[s % 2], xl[s % 2]), ((1,), (1,))
-            )
-
-        tiles(2, body)
+        step = split(full[s, p])
+        rest[p * chunk : (p + 1) * chunk, :] -= dot3(step, (xh[s % 2], xl[s % 2]), ((1,), (1,)))
 
     gram.scatter()
     tiles(tg // TILE, turn)
     cut(0)
     gram.finish(lambda v: v)
     for p in range(CHUNKS):
-        product(0, p, 1 - c)
-        product(0, p, c)
+        product(0, p)
     gram.collect()
     if nb > 2:
         block_copy(2).start()
@@ -354,9 +345,8 @@
                 hand_over(s, p)
             update(s, p)
             if not last:
-                product(s + 1, p, 1 - c)
+                product(s + 1, p)
                 sums[s + 1][p].swap()
-                product(s + 1, p, c)
                 sums[s + 1][p].scatter()
                 hand_over(s, p)
         if s > 1:

time: 234 us -> 233 us (level)
  no operation moved by 1% of the time
where the time goes in v4:
time: 233 us; the launch traced here: 229 us
  Pallas kernels  222 us (95%)
  local copies, waits for them, and re-layouts  6.17 us (3%)
    pallas_call x1, Pallas kernels, gathered(): pl.pallas_call(functools.partial(sweep_kernel, nb, nrows), out_shape=(jax...  222 us
    unnamed x4, local copies, waits for them, and re-layouts  6.17 us

profile of v4, /device:TPU:0, one launch (start us, length us, event | category | flops | bytes accessed | tf_op | source)
XLA Modules:
  0.0 229.1 jit_solution(16485295070220941165)
XLA Ops:
  0.6 222.3 %shard_map.41 = (f32[512,2048]{1,0:T(8,128)}, f32[1024,512]{1,0:T(8,128)}) custom-call(f32[1024,512]{1,0:T(8,128)} %x_ref.1, f32[1024,512]{1,0:T(8,128)} %t_ref.1), custom_call_target="tpu_custom_call" | custom-call | tf_op jit(solution)/shard_map/pallas_call | solution.py:386
  222.9 0.0 copy-start
  222.9 4.8 %copy.6 = f32[512,2048]{1,0:T(8,128)} copy(f32[512,2048]{1,0:T(8,128)} %get-tuple-element.4) | data formatting | bytes 8388608
  227.8 0.0 copy-done
  227.8 1.3 copy.7
Async XLA Ops:
  222.9 4.9 %copy-start = (f32[1024,512]{1,0:T(8,128)S(1)}, f32[1024,512]{1,0:T(8,128)}, u32[]{:S(2)}) copy-start(f32[1024,512]{1,0:T(8,128)} %get-tuple-element.5) | copy-start | bytes 6291460
